TPU v7x, 256 devices: a whole 4x4x8 slice. The times are simulated.
256 devices in a mesh: row: 4 (over y), col: 16 (over x, z_hi), rep: 4 (over z_lo, core).
Axes of the slice: x: 4, y: 4, z: 8 (z_hi: 4, z_lo: 2; z = z_hi * 2 + z_lo), core: 2. Of those that a mesh axis runs over, the one named last changes fastest.
Arguments:
- a_weights: bfloat16 [4, 4096, 2048], P('rep', 'row', 'col'), may hold values from 0 to 10000, as said below
- a_flags: int32 [4, 32, 16], P('rep', 'row', 'col'), may hold values 0 or 1
- b_weights: bfloat16 [4, 2048, 32768], P('rep', 'row', 'col'), may hold values from 0 to 10000, as said below
- b_flags: int32 [4, 16, 256], P('rep', 'row', 'col'), may hold values 0 or 1
- out_flags: int32 [32, 256], P('row', ('col', 'rep')), may hold values 0 or 1
Outputs:
- two_hop: bfloat16 [4096, 32768], P('row', ('col', 'rep'))
Inputs may be any that keep to these rules, and one draw needn't show every extreme that they name: `a_weights`: positive edge weights. `b_weights`: positive edge weights.
All inputs are finite; a program needn't handle non-finite values. No bound on the sum of `a_flags` or of `b_flags` or of `out_flags` on one device may be relied on, other than what follows from the above.
Results may differ from a plain program's by a relative error of at most 0.012.
Values may be sent and summed in bfloat16 or wider, within the bound.
No kernel may reach another device: no remote copies, remote signals or barrier semaphores. Data moves between devices by JAX's collectives and lax.ppermute only.
A program may use at most 64 MiB of HBM per device.

v0:
```python
import jax
import jax.numpy as jnp
from jax import lax
from jax.sharding import PartitionSpec as P


def expand(flags, width):
    return jnp.repeat(jnp.repeat(flags, width, axis=-2), width, axis=-1)


def shards(a_weights, a_flags, b_weights, b_flags, out_flags):
    width = a_weights.shape[1] // a_flags.shape[1]
    a_masked = a_weights * expand(a_flags, width).astype(jnp.bfloat16)
    b_masked = b_weights * expand(b_flags, width).astype(jnp.bfloat16)
    deg_a = 1.0 + lax.psum(jnp.sum(a_masked, axis=(0, 2), dtype=jnp.float32), ("col", "rep"))
    walk_local = (a_masked.astype(jnp.float32) / deg_a[None, :, None]).astype(jnp.bfloat16)
    walk_a = lax.all_gather(walk_local, "col", axis=2, tiled=True)
    deg_b = 1.0 + lax.psum(jnp.sum(b_masked, axis=2, dtype=jnp.float32), "col")
    walk_b = (b_masked.astype(jnp.float32) / deg_b[:, :, None]).astype(jnp.bfloat16)
    left_rows = walk_a[0]
    partial_sum = jnp.dot(
        left_rows,
        lax.all_gather(walk_b, "row", axis=1, tiled=True)[0],
        preferred_element_type=jnp.float32,
    )
    summed = lax.psum_scatter(
        partial_sum.astype(jnp.bfloat16), "rep", scatter_dimension=1, tiled=True
    ).astype(jnp.float32)
    factor = jnp.float32(b_weights.shape[2] * lax.axis_size("col"))
    return (factor * summed * expand(out_flags, width).astype(jnp.float32)).astype(jnp.bfloat16)


def solution(mesh):
    return jax.shard_map(
        shards,
        mesh=mesh,
        in_specs=(
            P("rep", "row", "col"),
            P("rep", "row", "col"),
            P("rep", "row", "col"),
            P("rep", "row", "col"),
            P("row", ("col", "rep")),
        ),
        out_specs=P("row", ("col", "rep")),
        check_vma=False,
    )
```

profile of v0, /device:TPU:1, one launch (start us, length us, event | category | flops | bytes accessed | tf_op | source)
XLA Modules:
  0.0 379.0 jit_solution(2328880365797852931)
XLA Ops:
  6.5 0.0 all-gather.3.cloned.1.call-start
  6.5 0.7 convert_bitcast_fusion.1
  7.2 0.1 broadcast_bitcast_fusion
  7.3 1.3 convert_reduce_fusion.1
  8.6 128.0 %psum.14 = f32[1024]{0:T(1024)S(1)} all-reduce(f32[1024]{0:T(1024)S(1)} %convert_reduce_fusion.1), channel_id=1, replica_groups=mesh['row'=4,'col'=16,'rep'=4] {'col','rep'}, use_global_device_ids=true, to_apply=%region_1.0 | all-reduce | flops 1024 | bytes 8192 | tf_op jit(solution)/shard_map/psum | solution.py:15
  136.6 2.0 fusion.10
  138.6 0.0 all-gather.3.cloned.1.call-update
  138.6 0.0 all-gather.5.cloned.1.call-start
  138.7 0.7 convert_bitcast_fusion
  139.4 2.3 broadcast_in_dim.20
  141.7 2.8 convert_element_type.80
  144.5 2.2 convert_reduce_fusion
  146.7 33.6 %psum.15 = f32[1,512]{1,0:T(1,128)S(1)} all-reduce(f32[1,512]{1,0:T(1,128)S(1)} %bitcast.29), channel_id=1, replica_groups=mesh['row'=4,'col'=16,'rep'=4] {'col'}, use_global_device_ids=true, to_apply=%region_3.0 | all-reduce | flops 512 | bytes 4096 | tf_op jit(solution)/shard_map/psum | solution.py:18
  180.3 3.9 %fusion.2 = bf16[1,512,2048]{2,1,0:T(8,128)(2,1)} fusion(f32[512]{0:T(512)S(1)} %bitcast.28, bf16[1,512,2048]{2,1,0:T(8,128)(2,1)} %param.7, bf16[1,512,2048]{2,1,0:T(8,128)(2,1)S(1)} %convert_element_type.80), kind=kLoop, calls=%fused_computation.4 | loop fusion | flops 4194304 | bytes 6293504 | tf_op jit(solution)/shard_map/convert_element_type | solution.py:19
  184.2 0.0 all-gather.5.cloned.1.call-update
  184.2 0.0 reduce-scatter.2.cloned.1.call-start
  184.3 36.4 %all-gather.3.cloned.1.call-done = bf16[1,1024,2048]{2,1,0:T(8,128)(2,1)} async-done(((bf16[1,1024,128]{2,1,0:T(8,128)(2,1)}), bf16[1,1024,2048]{2,1,0:T(8,128)(2,1)}) %all-gather.3.cloned.1.call-update) | async-done | bytes 4194320 | tf_op jit(solution)/shard_map/all_gather | solution.py:17
  220.6 86.0 %all-gather.5.cloned.1.call-done = bf16[1,2048,2048]{2,1,0:T(8,128)(2,1)} async-done(((bf16[1,512,2048]{2,1,0:T(8,128)(2,1)}), bf16[1,2048,2048]{2,1,0:T(8,128)(2,1)}) %all-gather.5.cloned.1.call-update) | async-done | bytes 8388624 | tf_op jit(solution)/shard_map/all_gather | solution.py:23
  306.6 13.8 %fusion.4 = bf16[1024,2048]{1,0:T(8,128)(2,1)} fusion(bf16[1,2048,2048]{2,1,0:T(8,128)(2,1)} %all-gather.5.cloned.1.call-done, bf16[1,1024,2048]{2,1,0:T(8,128)(2,1)} %all-gather.3.cloned.1.call-done), kind=kOutput, calls=%fused_computation.6 | convolution fusion | flops 8592031744 | bytes 16777216 | tf_op jit(solution)/shard_map/dot_general | solution.py:21
  320.4 0.0 copy-start.1
  320.4 0.0 reduce-scatter.2.cloned.1.call-update
  320.4 0.7 copy-done.1
  321.1 0.1 copy.6
  321.2 48.7 %reduce-scatter.2.cloned.1.call-done = bf16[1024,512]{1,0:T(8,128)(2,1)} async-done(((bf16[1024,2048]{1,0:T(8,128)(2,1)}), bf16[1024,512]{1,0:T(8,128)(2,1)}) %reduce-scatter.2.cloned.1.call-update) | async-done | bytes 1048592 | tf_op jit(solution)/shard_map/reduce_scatter | solution.py:26
  369.8 0.0 copy-start
  369.9 1.2 broadcast_in_dim.22
  371.1 0.0 copy-done
  371.1 1.4 fusion.9
  (5 shorter events, 0.1 us)
Async XLA Ops:
  6.5 214.1 %all-gather.3.cloned.1.call-start = ((), (), s32[]{:S(2)}) async-start(), calls=%async_computation.1 | async-start | bytes 4456448 | tf_op jit(solution)/shard_map/all_gather | solution.py:17
  138.6 168.0 %all-gather.5.cloned.1.call-start = ((), (), s32[]{:S(2)}) async-start(), calls=%async_computation.2 | async-start | bytes 10485760 | tf_op jit(solution)/shard_map/all_gather | solution.py:23
  184.2 185.6 %reduce-scatter.2.cloned.1.call-start = ((), (), s32[]{:S(2)}) async-start(), calls=%async_computation.3 | async-start | bytes 5242880 | tf_op jit(solution)/shard_map/reduce_scatter | solution.py:26
  320.4 0.7 copy-start.1
  369.8 1.3 copy-start
Sparse Core Ops, SparseCore 0:
  138.7 81.8 all-gather.2
  222.4 84.1 all-gather.4
  320.6 49.2 reduce-scatter.1
where the time goes:
time: 379 us
  waiting for transfers between devices  171 us (45%)
  blocking collectives  162 us (43%)
  matrix products  13.8 us (4%)
  between operations  13.1 us (3%)
  other arithmetic  12.1 us (3%)
  local copies, waits for them, and re-layouts  7.21 us (2%)
    psum x1, blocking collectives, shards(): lax.psum(jnp.sum(a_masked, axis=(0, 2), dtype=jnp.float32), ('col', 'rep'))  128 us
    all_gather x1, waiting for transfers between devices, shards(): lax.all_gather(walk_b, 'row', axis=1, tiled=True)[0]  86 us
    reduce_scatter x1, waiting for transfers between devices, shards(): lax.psum_scatter(partial_sum.astype(jnp.bfloat16), 'rep', scatter_dimensi...  48.7 us
    all_gather x1, waiting for transfers between devices, shards(): walk_a = lax.all_gather(walk_local, 'col', axis=2, tiled=True)  36.4 us
    psum x1, blocking collectives, shards(): deg_b = 1.0 + lax.psum(jnp.sum(b_masked, axis=2, dtype=jnp.float32), 'col')  33.6 us
    dot_general x1, matrix products, shards(): jnp.dot(left_rows, lax.all_gather(walk_b, 'row', axis=1, tiled=True)[0],...  13.8 us
  transfers between devices with their start and end apart: 3, of which 3 were waited for; matrix products, arithmetic and copies ran while one was open for 3% of the time, Pallas kernels for 0%

commit v1 on v0

--- a/solution.py
+++ b/solution.py
@@ -12,7 +12,9 @@
     width = a_weights.shape[1] // a_flags.shape[1]
     a_masked = a_weights * expand(a_flags, width).astype(jnp.bfloat16)
     b_masked = b_weights * expand(b_flags, width).astype(jnp.bfloat16)
-    deg_a = 1.0 + lax.psum(jnp.sum(a_masked, axis=(0, 2), dtype=jnp.float32), ("col", "rep"))
+    deg_a = 1.0 + lax.psum(
+        lax.psum(jnp.sum(a_masked, axis=(0, 2), dtype=jnp.float32), "col"), "rep"
+    )
     walk_local = (a_masked.astype(jnp.float32) / deg_a[None, :, None]).astype(jnp.bfloat16)
     walk_a = lax.all_gather(walk_local, "col", axis=2, tiled=True)
     deg_b = 1.0 + lax.psum(jnp.sum(b_masked, axis=2, dtype=jnp.float32), "col")

time: 379 us -> 307 us (0.81)
  blocking collectives: 162 us -> 54.6 us
  waiting for transfers between devices: 171 us -> 208 us
    psum x1, blocking collectives: 128 us -> 12.7 us  [shards(): lax.psum(lax.psum(jnp.sum(a_masked, axis=(0, 2), dtype=jnp.float32), 'col...]
    all_gather x1, waiting for transfers between devices: 36.4 us -> 73.3 us  [shards(): walk_a = lax.all_gather(walk_local, 'col', axis=2, tiled=True)]
    psum x1, blocking collectives: 33.6 us -> 41.9 us  [shards(): deg_b = 1.0 + lax.psum(jnp.sum(b_masked, axis=2, dtype=jnp.float32), 'col')]
  transfers between devices with their start and end apart: 3 -> 3, of which waited for: 3 -> 3; matrix products, arithmetic and copies ran while one was open for 3% -> 1% of each run, Pallas kernels for 0% -> 0%
where the time goes in v1:
time: 307 us; the launch traced here: 306 us
  waiting for transfers between devices  208 us (68%)
  blocking collectives  54.6 us (18%)
  matrix products  13.8 us (4%)
  between operations  13.2 us (4%)
  other arithmetic  9.64 us (3%)
  local copies, waits for them, and re-layouts  7.22 us (2%)
    all_gather x1, waiting for transfers between devices, shards(): lax.all_gather(walk_b, 'row', axis=1, tiled=True)[0]  85.8 us
    all_gather x1, waiting for transfers between devices, shards(): walk_a = lax.all_gather(walk_local, 'col', axis=2, tiled=True)  73.3 us
    reduce_scatter x1, waiting for transfers between devices, shards(): lax.psum_scatter(partial_sum.astype(jnp.bfloat16), 'rep', scatter_dimensi...  48.7 us
    psum x1, blocking collectives, shards(): deg_b = 1.0 + lax.psum(jnp.sum(b_masked, axis=2, dtype=jnp.float32), 'col')  41.9 us
    dot_general x1, matrix products, shards(): jnp.dot(left_rows, lax.all_gather(walk_b, 'row', axis=1, tiled=True)[0],...  13.8 us
    psum x1, blocking collectives, shards(): lax.psum(lax.psum(jnp.sum(a_masked, axis=(0, 2), dtype=jnp.float32), 'col...  12.7 us
  transfers between devices with their start and end apart: 3, of which 3 were waited for; matrix products, arithmetic and copies ran while one was open for 1% of the time, Pallas kernels for 0%

profile of v1, /device:TPU:1, one launch (start us, length us, event | category | flops | bytes accessed | tf_op | source)
XLA Modules:
  0.0 306.3 jit_solution(12393437691834775146)
XLA Ops:
  6.5 0.0 all-gather.3.cloned.1.call-start
  6.5 0.7 convert_bitcast_fusion
  7.2 2.3 broadcast_in_dim.20
  9.5 0.0 copy-start.3
  9.5 2.8 convert_element_type.80
  12.4 0.0 copy-done.3
  12.4 0.1 broadcast_bitcast_fusion
  12.5 0.0 copy-start
  12.5 2.3 convert_reduce_fusion
  14.7 0.0 copy-done
  14.7 0.4 convert_reduce_fusion.1
  15.1 41.9 %all-reduce = (f32[1,512]{1,0:T(1,128)S(1)}, f32[1024]{0:T(1024)S(1)}) all-reduce(f32[1,512]{1,0:T(1,128)S(1)} %bitcast.28, f32[1024]{0:T(1024)S(1)} %convert_reduce_fusion.1), channel_id=1, replica_groups=mesh['row'=4,'col'=16,'rep'=4] {'col'}, use_global_device_ids=true, to_apply=%region_4.0 | all-reduce | flops 1536 | bytes 12288 | tf_op jit(solution)/shard_map/psum | solution.py:20
  57.0 12.7 %psum.22 = f32[1024]{0:T(1024)S(1)} all-reduce(f32[1024]{0:T(1024)S(1)} %get-tuple-element.6), channel_id=1, replica_groups=mesh['row'=4,'col'=16,'rep'=4] {'rep'}, use_global_device_ids=true, to_apply=%region_2.0 | all-reduce | flops 1024 | bytes 8192 | tf_op jit(solution)/shard_map/psum | solution.py:15
  69.7 1.0 fusion.10
  70.7 0.0 all-gather.3.cloned.1.call-update
  70.7 0.0 all-gather.5.cloned.1.call-start
  70.8 3.9 %fusion.2 = bf16[1,512,2048]{2,1,0:T(8,128)(2,1)} fusion(f32[512]{0:T(512)S(1)} %bitcast.29, bf16[1,512,2048]{2,1,0:T(8,128)(2,1)} %param.7, bf16[1,512,2048]{2,1,0:T(8,128)(2,1)S(1)} %convert_element_type.80), kind=kLoop, calls=%fused_computation.4 | loop fusion | flops 4194304 | bytes 6293504 | tf_op jit(solution)/shard_map/convert_element_type | solution.py:21
  74.7 0.0 all-gather.5.cloned.1.call-update
  74.7 0.0 reduce-scatter.2.cloned.1.call-start
  74.8 73.3 %all-gather.3.cloned.1.call-done = bf16[1,1024,2048]{2,1,0:T(8,128)(2,1)} async-done(((bf16[1,1024,128]{2,1,0:T(8,128)(2,1)}), bf16[1,1024,2048]{2,1,0:T(8,128)(2,1)}) %all-gather.3.cloned.1.call-update) | async-done | bytes 4194320 | tf_op jit(solution)/shard_map/all_gather | solution.py:19
  148.0 85.8 %all-gather.5.cloned.1.call-done = bf16[1,2048,2048]{2,1,0:T(8,128)(2,1)} async-done(((bf16[1,512,2048]{2,1,0:T(8,128)(2,1)}), bf16[1,2048,2048]{2,1,0:T(8,128)(2,1)}) %all-gather.5.cloned.1.call-update) | async-done | bytes 8388624 | tf_op jit(solution)/shard_map/all_gather | solution.py:25
  233.9 13.8 %fusion.4 = bf16[1024,2048]{1,0:T(8,128)(2,1)} fusion(bf16[1,2048,2048]{2,1,0:T(8,128)(2,1)} %all-gather.5.cloned.1.call-done, bf16[1,1024,2048]{2,1,0:T(8,128)(2,1)} %all-gather.3.cloned.1.call-done), kind=kOutput, calls=%fused_computation.6 | convolution fusion | flops 8592031744 | bytes 16777216 | tf_op jit(solution)/shard_map/dot_general | solution.py:23
  247.7 0.0 copy-start.2
  247.7 0.0 reduce-scatter.2.cloned.1.call-update
  247.7 0.7 copy-done.2
  248.4 0.1 copy.6
  248.4 48.7 %reduce-scatter.2.cloned.1.call-done = bf16[1024,512]{1,0:T(8,128)(2,1)} async-done(((bf16[1024,2048]{1,0:T(8,128)(2,1)}), bf16[1024,512]{1,0:T(8,128)(2,1)}) %reduce-scatter.2.cloned.1.call-update) | async-done | bytes 1048592 | tf_op jit(solution)/shard_map/reduce_scatter | solution.py:28
  297.1 0.0 copy-start.1
  297.1 1.2 broadcast_in_dim.22
  298.4 0.0 copy-done.1
  298.4 1.4 fusion.9
  (6 shorter events, 0.1 us)
Async XLA Ops:
  6.5 141.5 %all-gather.3.cloned.1.call-start = ((), (), s32[]{:S(2)}) async-start(), calls=%async_computation.1 | async-start | bytes 4456448 | tf_op jit(solution)/shard_map/all_gather | solution.py:19
  9.5 2.8 copy-start.3
  12.5 2.3 copy-start
  70.7 163.1 %all-gather.5.cloned.1.call-start = ((), (), s32[]{:S(2)}) async-start(), calls=%async_computation.2 | async-start | bytes 10485760 | tf_op jit(solution)/shard_map/all_gather | solution.py:25
  74.7 222.4 %reduce-scatter.2.cloned.1.call-start = ((), (), s32[]{:S(2)}) async-start(), calls=%async_computation.3 | async-start | bytes 5242880 | tf_op jit(solution)/shard_map/reduce_scatter | solution.py:28
  247.7 0.7 copy-start.2
  297.1 1.3 copy-start.1
Sparse Core Ops, SparseCore 0:
  70.9 77.1 all-gather.2
  149.8 83.9 all-gather.4
  247.8 49.2 reduce-scatter.1
